TPU v7x, 512 devices: a whole 4x4x16 slice. The times are simulated.
512 devices in a mesh: pair: 32 (over y, z_lo), row: 16 (over z_hi, x, core).
Axes of the slice: x: 4, y: 4, z: 16 (z_hi: 2, z_lo: 8; z = z_hi * 8 + z_lo), core: 2. Of those that a mesh axis runs over, the one named last changes fastest.
Arguments:
- factor: float32 [8192, 16384], P('row', 'pair'), may hold values from -6 to 6
- plan: int32 [2, 512], replicated, may hold values from 0 to 511, each once within a row
Outputs:
- rotated: float32 [8192, 16384], P('row', 'pair')
Inputs may be any that keep to these rules, and one draw needn't show every extreme that they name: Each row of plan names every number of 0 to 511 once.
All inputs are finite; a program needn't handle non-finite values.
Results may differ from a plain program's by a relative error of at most 0.0001.
Values sent between devices are 32-bit elements; how exact they have to be, the bound alone decides.
A program may use at most 64 MiB of HBM per device.

v0:
```python
import jax
import jax.numpy as jnp
from jax import lax
from jax.sharding import PartitionSpec as P

BLK = 256
ROUNDS = 2
NS_STEPS = 3
eps_value = 1e-06


def from_behind(value, axis, by):
    devices = lax.axis_size(axis)
    return lax.ppermute(value, axis, [(i, (i + by) % devices) for i in range(devices)])


def product(left, right):
    return jnp.dot(left, right, precision=lax.Precision.HIGHEST, preferred_element_type=jnp.float32)


def sign_table(width, col_ids):
    rows_idx = jnp.arange(width)[:, None]
    cols_idx = col_ids[None, :]
    positive = (rows_idx < BLK) & (cols_idx >= BLK)
    negative = (rows_idx >= BLK) & (cols_idx < BLK)
    sign = jnp.where(positive, 1.0, jnp.where(negative, -1.0, 0.0)).astype(jnp.float32)
    unit = (rows_idx == cols_idx).astype(jnp.float32)
    return (sign, positive, unit)


def shards(factor, plan):
    width = factor.shape[1]
    blocks = factor
    for rnd in range(ROUNDS):
        work = jnp.take(blocks, plan[rnd], axis=1)
        partial_value = product(work.T, work)
        groups = lax.axis_size("row")
        count = width // groups
        half = count // 2
        device = lax.axis_index("row")
        spot = jnp.arange(count)
        own_ids = spot // half * BLK + device * half + spot % half
        mixed = (
            partial_value.reshape(width, 2, groups, half)
            .transpose(0, 2, 1, 3)
            .reshape(width, width)
        )
        columns = lax.psum_scatter(mixed, "row", scatter_dimension=1, tiled=True)
        own_block = jnp.take(columns, own_ids, axis=0)
        own_diag = jnp.diagonal(own_block)
        gathered = lax.all_gather(own_diag, "row", axis=0, tiled=True)
        diag = gathered.reshape(groups, 2, half).transpose(1, 0, 2).reshape(width)
        inverse = 1.0 / jnp.sqrt(diag + eps_value)
        own_inverse = 1.0 / jnp.sqrt(own_diag + eps_value)
        normed = columns * inverse[:, None] * own_inverse[None, :]
        sign, positive, unit = sign_table(width, own_ids)
        local_sq = jnp.sum(jnp.where(positive, normed * normed, 0.0))
        total = lax.psum(local_sq, "row")
        scale = 1.0 / (1.0 + jnp.sqrt(total))
        iterate = unit + sign * normed * scale
        for step in range(NS_STEPS):
            current = iterate
            piece = lax.all_gather(current, "row", axis=1, tiled=True)
            folded = product(piece, product(piece.T, current))
            iterate = 1.5 * current - 0.5 * folded
        turned = product(work, lax.all_gather(iterate, "row", axis=1, tiled=True))
        work = turned.reshape(-1, groups, 2, half).transpose(0, 2, 1, 3).reshape(-1, width)
        second = from_behind(work[:, BLK:], "pair", 1)
        blocks = jnp.concatenate([work[:, :BLK], second], axis=1)
    return blocks


def solution(mesh):
    placed = (P("row", "pair"), P())
    return jax.shard_map(
        shards, mesh=mesh, in_specs=placed, out_specs=P("row", "pair"), check_vma=False
    )
```

profile of v0, /device:TPU:1, one launch (start us, length us, event | category | flops | bytes accessed | tf_op | source)
XLA Modules:
  0.0 1138.3 jit_solution(16740906257814945387)
XLA Ops:
  6.5 0.8 fusion.37
  7.3 1.6 copy.18
  8.9 1.6 gather_fusion.2
  10.5 2.0 fusion.12
  12.6 1.0 copy.19
  13.7 1.3 dynamic-slice
  15.7 109.5 %reduce-scatter.3.cloned.1.call-done = f32[512,32]{0,1:T(8,128)} async-done(((f32[512,512]{0,1:T(8,128)}), f32[512,32]{0,1:T(8,128)}) %reduce-scatter.3.cloned.1.call-update) | async-done | bytes 65552 | tf_op jit(solution)/shard_map/reduce_scatter | solution.py:48
  125.2 1.0 copy.20
  126.8 0.7 gather_fusion
  127.8 63.5 %all-reduce = f32[512]{0:T(512)S(1)} all-reduce(f32[512]{0:T(512)S(1)} %dynamic-update-slice), channel_id=1, replica_groups=mesh['pair'=32,'row'=16] {'row'}, use_global_device_ids=true, to_apply=%add | all-reduce | flops 512 | bytes 4096
  192.3 62.6 %psum.14 = f32[]{:T(128)} all-reduce(f32[]{:T(128)} %fusion.26), channel_id=1, replica_groups=mesh['pair'=32,'row'=16] {'row'}, use_global_device_ids=true, to_apply=%region_2.5 | all-reduce | flops 1 | bytes 8 | tf_op jit(solution)/shard_map/psum | solution.py:58
  255.6 0.7 convert_add_fusion.1
  256.4 76.3 %all-gather.9.cloned.1.call-done = f32[512,512]{0,1:T(8,128)} async-done(((f32[512,32]{0,1:T(8,128)}), f32[512,512]{0,1:T(8,128)}) %all-gather.9.cloned.1.call-update) | async-done | bytes 1048592 | tf_op jit(solution)/shard_map/all_gather | solution.py:63
  332.7 2.4 fusion.38
  335.1 1.4 fusion.5
  336.6 68.6 %all-gather.11.cloned.1.call-done = f32[512,512]{0,1:T(8,128)} async-done(((f32[512,32]{0,1:T(8,128)}), f32[512,512]{0,1:T(8,128)}) %all-gather.11.cloned.1.call-update) | async-done | bytes 1048592 | tf_op jit(solution)/shard_map/all_gather | solution.py:63
  405.2 2.4 fusion.39
  407.6 1.4 fusion.4
  409.0 68.6 %all-gather.13.cloned.1.call-done = f32[512,512]{0,1:T(8,128)} async-done(((f32[512,32]{0,1:T(8,128)}), f32[512,512]{0,1:T(8,128)}) %all-gather.13.cloned.1.call-update) | async-done | bytes 1048592 | tf_op jit(solution)/shard_map/all_gather | solution.py:63
  477.6 2.4 fusion.40
  480.0 1.4 fusion.3
  481.5 68.6 %all-gather.15.cloned.1.call-done = f32[512,512]{0,1:T(8,128)} async-done(((f32[512,32]{0,1:T(8,128)}), f32[512,512]{0,1:T(8,128)}) %all-gather.15.cloned.1.call-update) | async-done | bytes 1048592 | tf_op jit(solution)/shard_map/all_gather | solution.py:66
  550.1 3.2 fusion.10
  553.5 2.1 collective-permute-start
  555.6 21.7 %collective-permute-done = f32[512,256]{0,1:T(8,128)S(1)} collective-permute-done((f32[512,256]{0,1:T(8,128)S(1)}, f32[512,256]{0,1:T(8,128)S(1)}, u32[]{:S(2)}, u32[]{:S(2)}) %collective-permute-start) | collective-permute-done | bytes 524320 | tf_op jit(solution)/shard_map/ppermute | solution.py:14
  577.4 1.6 gather_fusion.4
  579.0 2.0 fusion.8
  581.0 1.0 copy.23
  582.1 95.9 %reduce-scatter.5.cloned.1.call-done = f32[512,32]{0,1:T(8,128)} async-done(((f32[512,512]{0,1:T(8,128)}), f32[512,32]{0,1:T(8,128)}) %reduce-scatter.5.cloned.1.call-update) | async-done | bytes 65552 | tf_op jit(solution)/shard_map/reduce_scatter | solution.py:48
  678.1 1.0 copy.24
  679.7 0.7 gather_fusion.1
  680.7 63.6 %all-reduce.1 = f32[512]{0:T(512)S(1)} all-reduce(f32[512]{0:T(512)S(1)} %dynamic-update-slice.1), channel_id=1, replica_groups=mesh['pair'=32,'row'=16] {'row'}, use_global_device_ids=true, to_apply=%add.1 | all-reduce | flops 512 | bytes 4096
  745.1 62.6 %psum.15 = f32[]{:T(128)} all-reduce(f32[]{:T(128)} %fusion.27), channel_id=1, replica_groups=mesh['pair'=32,'row'=16] {'row'}, use_global_device_ids=true, to_apply=%region_5.8 | all-reduce | flops 1 | bytes 8 | tf_op jit(solution)/shard_map/psum | solution.py:58
  808.5 0.7 convert_add_fusion
  809.3 76.3 %all-gather.17.cloned.1.call-done = f32[512,512]{0,1:T(8,128)} async-done(((f32[512,32]{0,1:T(8,128)}), f32[512,512]{0,1:T(8,128)}) %all-gather.17.cloned.1.call-update) | async-done | bytes 1048592 | tf_op jit(solution)/shard_map/all_gather | solution.py:63
  885.6 2.4 fusion.41
  887.9 1.4 fusion.2
  889.4 68.6 %all-gather.19.cloned.1.call-done = f32[512,512]{0,1:T(8,128)} async-done(((f32[512,32]{0,1:T(8,128)}), f32[512,512]{0,1:T(8,128)}) %all-gather.19.cloned.1.call-update) | async-done | bytes 1048592 | tf_op jit(solution)/shard_map/all_gather | solution.py:63
  958.0 2.4 fusion.42
  960.4 1.4 fusion.1
  961.8 68.6 %all-gather.21.cloned.1.call-done = f32[512,512]{0,1:T(8,128)} async-done(((f32[512,32]{0,1:T(8,128)}), f32[512,512]{0,1:T(8,128)}) %all-gather.21.cloned.1.call-update) | async-done | bytes 1048592 | tf_op jit(solution)/shard_map/all_gather | solution.py:63
  1030.5 2.4 fusion.43
  1032.8 1.4 fusion
  1034.2 68.7 %all-gather.23.cloned.1.call-done = f32[512,512]{0,1:T(8,128)} async-done(((f32[512,32]{0,1:T(8,128)}), f32[512,512]{0,1:T(8,128)}) %all-gather.23.cloned.1.call-update) | async-done | bytes 1048592 | tf_op jit(solution)/shard_map/all_gather | solution.py:66
  1102.9 3.2 fusion.6
  1106.3 1.9 collective-permute-start.1
  1108.2 21.9 %collective-permute-done.1 = f32[512,256]{0,1:T(8,128)S(1)} collective-permute-done((f32[512,256]{0,1:T(8,128)S(1)}, f32[512,256]{0,1:T(8,128)S(1)}, u32[]{:S(2)}, u32[]{:S(2)}) %collective-permute-start.1) | collective-permute-done | bytes 524320 | tf_op jit(solution)/shard_map/ppermute | solution.py:14
  1130.2 1.3 copy.27
  (87 shorter events, 4.7 us)
Async XLA Ops:
  6.5 118.7 %reduce-scatter.3.cloned.1.call-start = ((), (), s32[]{:S(2)}) async-start(), calls=%async_computation.2 | async-start | bytes 1114112 | tf_op jit(solution)/shard_map/reduce_scatter | solution.py:48
  13.6 319.1 %all-gather.9.cloned.1.call-start = ((), (), s32[]{:S(2)}) async-start(), calls=%async_computation.3 | async-start | bytes 1114112 | tf_op jit(solution)/shard_map/all_gather | solution.py:63
  127.6 64.0 %copy-start.12 = (f32[512,32]{0,1:T(8,128)S(1)}, f32[512,32]{0,1:T(8,128)}, u32[]{:S(2)}) copy-start(f32[512,32]{0,1:T(8,128)} %reduce-scatter.3.cloned.1.call-done) | copy-start | bytes 196612
  256.3 76.4 %copy-start.11 = (f32[512,32]{0,1:T(8,128)S(1)}, f32[512,32]{0,1:T(8,128)}, u32[]{:S(2)}) copy-start(f32[512,32]{0,1:T(8,128)} %convert_add_fusion.1) | copy-start | bytes 196612
  256.4 148.8 %all-gather.11.cloned.1.call-start = ((), (), s32[]{:S(2)}) async-start(), calls=%async_computation.4 | async-start | bytes 1114112 | tf_op jit(solution)/shard_map/all_gather | solution.py:63
  332.7 2.4 copy-start
  336.5 68.7 %copy-start.6 = (f32[512,32]{0,1:T(8,128)S(1)}, f32[512,32]{0,1:T(8,128)}, u32[]{:S(2)}) copy-start(f32[512,32]{0,1:T(8,128)} %fusion.5) | copy-start | bytes 196612
  336.5 141.1 %all-gather.13.cloned.1.call-start = ((), (), s32[]{:S(2)}) async-start(), calls=%async_computation.5 | async-start | bytes 1114112 | tf_op jit(solution)/shard_map/all_gather | solution.py:63
  405.2 2.4 copy-start.1
  408.9 68.7 %copy-start.7 = (f32[512,32]{0,1:T(8,128)S(1)}, f32[512,32]{0,1:T(8,128)}, u32[]{:S(2)}) copy-start(f32[512,32]{0,1:T(8,128)} %fusion.4) | copy-start | bytes 196612
  409.0 141.1 %all-gather.15.cloned.1.call-start = ((), (), s32[]{:S(2)}) async-start(), calls=%async_computation.6 | async-start | bytes 1114112 | tf_op jit(solution)/shard_map/all_gather | solution.py:66
  477.6 2.4 copy-start.2
  481.4 196.7 %reduce-scatter.5.cloned.1.call-start = ((), (), s32[]{:S(2)}) async-start(), calls=%async_computation.7 | async-start | bytes 1114112 | tf_op jit(solution)/shard_map/reduce_scatter | solution.py:48
  553.5 23.8 %collective-permute-start = (f32[512,256]{0,1:T(8,128)S(1)}, f32[512,256]{0,1:T(8,128)S(1)}, u32[]{:S(2)}, u32[]{:S(2)}) collective-permute-start(f32[512,256]{0,1:T(8,128)S(1)} %get-tuple-element.10), channel_id=1, source_target_pairs={{0,16},{16,32},{32,48},{48,64},{64,80},{80,96},{96,112},{112,128},... | collective-permute-start | bytes 1572872 | tf_op jit(solution)/shard_map/ppermute | solution.py:14
  582.1 303.4 %all-gather.17.cloned.1.call-start = ((), (), s32[]{:S(2)}) async-start(), calls=%async_computation.8 | async-start | bytes 1114112 | tf_op jit(solution)/shard_map/all_gather | solution.py:63
  680.4 64.0 %copy-start.13 = (f32[512,32]{0,1:T(8,128)S(1)}, f32[512,32]{0,1:T(8,128)}, u32[]{:S(2)}) copy-start(f32[512,32]{0,1:T(8,128)} %reduce-scatter.5.cloned.1.call-done) | copy-start | bytes 196612
  809.2 76.4 %copy-start.10 = (f32[512,32]{0,1:T(8,128)S(1)}, f32[512,32]{0,1:T(8,128)}, u32[]{:S(2)}) copy-start(f32[512,32]{0,1:T(8,128)} %convert_add_fusion) | copy-start | bytes 196612
  809.2 148.8 %all-gather.19.cloned.1.call-start = ((), (), s32[]{:S(2)}) async-start(), calls=%async_computation.9 | async-start | bytes 1114112 | tf_op jit(solution)/shard_map/all_gather | solution.py:63
  885.6 2.4 copy-start.3
  889.3 68.7 %copy-start.8 = (f32[512,32]{0,1:T(8,128)S(1)}, f32[512,32]{0,1:T(8,128)}, u32[]{:S(2)}) copy-start(f32[512,32]{0,1:T(8,128)} %fusion.2) | copy-start | bytes 196612
  889.3 141.1 %all-gather.21.cloned.1.call-start = ((), (), s32[]{:S(2)}) async-start(), calls=%async_computation.10 | async-start | bytes 1114112 | tf_op jit(solution)/shard_map/all_gather | solution.py:63
  958.0 2.4 copy-start.4
  961.8 68.7 %copy-start.9 = (f32[512,32]{0,1:T(8,128)S(1)}, f32[512,32]{0,1:T(8,128)}, u32[]{:S(2)}) copy-start(f32[512,32]{0,1:T(8,128)} %fusion.1) | copy-start | bytes 196612
  961.8 141.1 %all-gather.23.cloned.1.call-start = ((), (), s32[]{:S(2)}) async-start(), calls=%async_computation.11 | async-start | bytes 1114112 | tf_op jit(solution)/shard_map/all_gather | solution.py:66
  1030.5 2.4 copy-start.5
  1106.3 23.8 %collective-permute-start.1 = (f32[512,256]{0,1:T(8,128)S(1)}, f32[512,256]{0,1:T(8,128)S(1)}, u32[]{:S(2)}, u32[]{:S(2)}) collective-permute-start(f32[512,256]{0,1:T(8,128)S(1)} %get-tuple-element.8), channel_id=1, source_target_pairs={{0,16},{16,32},{32,48},{48,64},{64,80},{80,96},{96,112},{112,128},... | collective-permute-start | bytes 1572872 | tf_op jit(solution)/shard_map/ppermute | solution.py:14
Sparse Core Ops, SparseCore 0:
  13.8 111.4 reduce-scatter.2
  256.5 76.1 all-gather.8
  336.6 68.5 all-gather.10
  409.1 68.4 all-gather.12
  481.5 68.4 all-gather.14
  582.2 95.7 reduce-scatter.4
  809.3 76.1 all-gather.16
  889.5 68.4 all-gather.18
  961.9 68.5 all-gather.20
  1034.3 68.4 all-gather.22
where the time goes:
time: 1140 us
  waiting for transfers between devices  813 us (71%)
  blocking collectives  252 us (22%)
  matrix products  32.9 us (3%)
  local copies, waits for them, and re-layouts  16 us (1%)
  between operations  16 us (1%)
    all_gather x6, waiting for transfers between devices, shards(): piece = lax.all_gather(current, 'row', axis=1, tiled=True)  427 us
    reduce_scatter x2, waiting for transfers between devices, shards(): columns = lax.psum_scatter(mixed, 'row', scatter_dimension=1, tiled=True)  205 us
    all_gather x2, waiting for transfers between devices, shards(): turned = product(work, lax.all_gather(iterate, 'row', axis=1, tiled=True))  137 us
    unnamed x2, blocking collectives  127 us
    psum x2, blocking collectives, shards(): total = lax.psum(local_sq, 'row')  125 us
    ppermute x2, waiting for transfers between devices, from_behind(): lax.ppermute(value, axis, [(i, (i + by) % devices) for i in range(devices)])  43.5 us
    dot_general x16, matrix products, product(): jnp.dot(left, right, precision=lax.Precision.HIGHEST, preferred_element_t...  32.9 us
  transfers between devices with their start and end apart: 12, of which 12 were waited for; matrix products, arithmetic and copies ran while one was open for 0% of the time, Pallas kernels for 0%

commit v1 on v0

--- a/solution.py
+++ b/solution.py
@@ -60,7 +60,9 @@
         iterate = unit + sign * normed * scale
         for step in range(NS_STEPS):
             current = iterate
-            piece = lax.all_gather(current, "row", axis=1, tiled=True)
+            piece = jnp.concatenate(
+                lax.all_to_all(jnp.stack([current] * lax.axis_size("row")), "row", 0, 0), axis=1
+            )
             folded = product(piece, product(piece.T, current))
             iterate = 1.5 * current - 0.5 * folded
         turned = product(work, lax.all_gather(iterate, "row", axis=1, tiled=True))

time: 1140 us -> 1030 us (0.904)
  waiting for transfers between devices: 813 us -> 394 us
  blocking collectives: 252 us -> 574 us
    all_gather x6 -> x0, waiting for transfers between devices: 427 us -> none  [shards(): piece = lax.all_gather(current, 'row', axis=1, tiled=True)]
    all_to_all x0 -> x6, blocking collectives: none -> 322 us  [shards(): lax.all_to_all(jnp.stack([current] * lax.axis_size('row')), 'row', 0, 0)]
  transfers between devices with their start and end apart: 12 -> 6, of which waited for: 12 -> 6; matrix products, arithmetic and copies ran while one was open for 0% -> 0% of each run, Pallas kernels for 0% -> 0%
where the time goes in v1:
time: 1030 us
  blocking collectives  574 us (56%)
  waiting for transfers between devices  394 us (38%)
  matrix products  22.6 us (2%)
  local copies, waits for them, and re-layouts  16.6 us (2%)
  between operations  15.7 us (2%)
    all_to_all x6, blocking collectives, shards(): lax.all_to_all(jnp.stack([current] * lax.axis_size('row')), 'row', 0, 0)  322 us
    reduce_scatter x2, waiting for transfers between devices, shards(): columns = lax.psum_scatter(mixed, 'row', scatter_dimension=1, tiled=True)  205 us
    all_gather x2, waiting for transfers between devices, shards(): turned = product(work, lax.all_gather(iterate, 'row', axis=1, tiled=True))  145 us
    unnamed x2, blocking collectives  127 us
    psum x2, blocking collectives, shards(): total = lax.psum(local_sq, 'row')  125 us
    ppermute x2, waiting for transfers between devices, from_behind(): lax.ppermute(value, axis, [(i, (i + by) % devices) for i in range(devices)])  43.5 us
    dot_general x16, matrix products, product(): jnp.dot(left, right, precision=lax.Precision.HIGHEST, preferred_element_t...  22.6 us
  transfers between devices with their start and end apart: 6, of which 6 were waited for; matrix products, arithmetic and copies ran while one was open for 0% of the time, Pallas kernels for 0%

profile of v1, /device:TPU:1, one launch (start us, length us, event | category | flops | bytes accessed | tf_op | source)
XLA Modules:
  0.0 1029.3 jit_solution(15536687301298049592)
XLA Ops:
  6.5 0.8 fusion.37
  7.3 1.6 copy.24
  8.9 1.6 gather_fusion.2
  10.5 2.0 fusion.12
  12.6 1.0 copy.25
  13.7 1.3 dynamic-slice
  15.8 109.5 %reduce-scatter.3.cloned.1.call-done = f32[512,32]{0,1:T(8,128)} async-done(((f32[512,512]{0,1:T(8,128)}), f32[512,32]{0,1:T(8,128)}) %reduce-scatter.3.cloned.1.call-update) | async-done | bytes 65552 | tf_op jit(solution)/shard_map/reduce_scatter | solution.py:48
  125.3 1.0 copy.26
  126.9 0.7 gather_fusion
  127.9 63.5 %all-reduce = f32[512]{0:T(512)S(1)} all-reduce(f32[512]{0:T(512)S(1)} %dynamic-update-slice), channel_id=1, replica_groups=mesh['pair'=32,'row'=16] {'row'}, use_global_device_ids=true, to_apply=%add | all-reduce | flops 512 | bytes 4096
  191.6 0.7 fusion.26
  192.3 62.6 %psum.14 = f32[]{:T(128)} all-reduce(f32[]{:T(128)} %fusion.26), channel_id=1, replica_groups=mesh['pair'=32,'row'=16] {'row'}, use_global_device_ids=true, to_apply=%region_2.5 | all-reduce | flops 1 | bytes 8 | tf_op jit(solution)/shard_map/psum | solution.py:58
  255.9 62.1 %all_to_all.30 = f32[16,512,32]{1,2,0:T(8,128)S(1)} all-to-all(f32[16,512,32]{1,2,0:T(8,128)S(1)} %stack.12), channel_id=1, replica_groups=mesh['pair'=32,'row'=16] {'row'}, dimensions={0} | all-to-all | bytes 2097152 | tf_op jit(solution)/shard_map/all_to_all | solution.py:64
  317.9 1.1 fusion.38
  319.0 0.7 fusion.5
  319.9 51.6 %all_to_all.31 = f32[16,512,32]{1,2,0:T(8,128)S(1)} all-to-all(f32[16,512,32]{1,2,0:T(8,128)S(1)} %stack.13), channel_id=1, replica_groups=mesh['pair'=32,'row'=16] {'row'}, dimensions={0} | all-to-all | bytes 2097152 | tf_op jit(solution)/shard_map/all_to_all | solution.py:64
  371.5 1.1 fusion.39
  372.6 0.7 fusion.4
  373.4 47.4 %all_to_all.32 = f32[16,512,32]{1,2,0:T(8,128)S(1)} all-to-all(f32[16,512,32]{1,2,0:T(8,128)S(1)} %stack.14), channel_id=1, replica_groups=mesh['pair'=32,'row'=16] {'row'}, dimensions={0} | all-to-all | bytes 2097152 | tf_op jit(solution)/shard_map/all_to_all | solution.py:64
  420.8 1.1 fusion.40
  421.9 1.4 fusion.3
  423.4 72.4 %all-gather.3.cloned.1.call-done = f32[512,512]{0,1:T(8,128)} async-done(((f32[512,32]{0,1:T(8,128)}), f32[512,512]{0,1:T(8,128)}) %all-gather.3.cloned.1.call-update) | async-done | bytes 1048592 | tf_op jit(solution)/shard_map/all_gather | solution.py:68
  495.7 3.2 fusion.10
  499.1 2.1 collective-permute-start
  501.3 21.7 %collective-permute-done = f32[512,256]{0,1:T(8,128)S(1)} collective-permute-done((f32[512,256]{0,1:T(8,128)S(1)}, f32[512,256]{0,1:T(8,128)S(1)}, u32[]{:S(2)}, u32[]{:S(2)}) %collective-permute-start) | collective-permute-done | bytes 524320 | tf_op jit(solution)/shard_map/ppermute | solution.py:14
  523.0 1.6 gather_fusion.4
  524.6 2.0 fusion.8
  526.7 1.0 copy.29
  527.8 96.0 %reduce-scatter.5.cloned.1.call-done = f32[512,32]{0,1:T(8,128)} async-done(((f32[512,512]{0,1:T(8,128)}), f32[512,32]{0,1:T(8,128)}) %reduce-scatter.5.cloned.1.call-update) | async-done | bytes 65552 | tf_op jit(solution)/shard_map/reduce_scatter | solution.py:48
  623.8 1.0 copy.30
  625.4 0.7 gather_fusion.1
  626.4 63.5 %all-reduce.1 = f32[512]{0:T(512)S(1)} all-reduce(f32[512]{0:T(512)S(1)} %dynamic-update-slice.1), channel_id=1, replica_groups=mesh['pair'=32,'row'=16] {'row'}, use_global_device_ids=true, to_apply=%add.1 | all-reduce | flops 512 | bytes 4096
  690.1 0.7 fusion.27
  690.8 62.6 %psum.15 = f32[]{:T(128)} all-reduce(f32[]{:T(128)} %fusion.27), channel_id=1, replica_groups=mesh['pair'=32,'row'=16] {'row'}, use_global_device_ids=true, to_apply=%region_5.8 | all-reduce | flops 1 | bytes 8 | tf_op jit(solution)/shard_map/psum | solution.py:58
  754.4 62.0 %all_to_all.33 = f32[16,512,32]{1,2,0:T(8,128)S(1)} all-to-all(f32[16,512,32]{1,2,0:T(8,128)S(1)} %stack.15), channel_id=1, replica_groups=mesh['pair'=32,'row'=16] {'row'}, dimensions={0} | all-to-all | bytes 2097152 | tf_op jit(solution)/shard_map/all_to_all | solution.py:64
  816.4 1.1 fusion.41
  817.5 0.7 fusion.2
  818.3 51.6 %all_to_all.34 = f32[16,512,32]{1,2,0:T(8,128)S(1)} all-to-all(f32[16,512,32]{1,2,0:T(8,128)S(1)} %stack.16), channel_id=1, replica_groups=mesh['pair'=32,'row'=16] {'row'}, dimensions={0} | all-to-all | bytes 2097152 | tf_op jit(solution)/shard_map/all_to_all | solution.py:64
  870.0 1.1 fusion.42
  871.1 0.7 fusion.1
  871.9 47.5 %all_to_all.35 = f32[16,512,32]{1,2,0:T(8,128)S(1)} all-to-all(f32[16,512,32]{1,2,0:T(8,128)S(1)} %stack.17), channel_id=1, replica_groups=mesh['pair'=32,'row'=16] {'row'}, dimensions={0} | all-to-all | bytes 2097152 | tf_op jit(solution)/shard_map/all_to_all | solution.py:64
  919.4 1.1 fusion.43
  920.4 1.4 fusion
  921.8 72.4 %all-gather.5.cloned.1.call-done = f32[512,512]{0,1:T(8,128)} async-done(((f32[512,32]{0,1:T(8,128)}), f32[512,512]{0,1:T(8,128)}) %all-gather.5.cloned.1.call-update) | async-done | bytes 1048592 | tf_op jit(solution)/shard_map/all_gather | solution.py:68
  994.2 3.2 fusion.6
  997.6 1.9 collective-permute-start.1
  999.5 21.9 %collective-permute-done.1 = f32[512,256]{0,1:T(8,128)S(1)} collective-permute-done((f32[512,256]{0,1:T(8,128)S(1)}, f32[512,256]{0,1:T(8,128)S(1)}, u32[]{:S(2)}, u32[]{:S(2)}) %collective-permute-start.1) | collective-permute-done | bytes 524320 | tf_op jit(solution)/shard_map/ppermute | solution.py:14
  1021.5 1.3 copy.33
  (57 shorter events, 3.8 us)
Async XLA Ops:
  6.5 118.8 %reduce-scatter.3.cloned.1.call-start = ((), (), s32[]{:S(2)}) async-start(), calls=%async_computation.8 | async-start | bytes 1114112 | tf_op jit(solution)/shard_map/reduce_scatter | solution.py:48
  13.6 482.1 %all-gather.3.cloned.1.call-start = ((), (), s32[]{:S(2)}) async-start(), calls=%async_computation.9 | async-start | bytes 1114112 | tf_op jit(solution)/shard_map/all_gather | solution.py:68
  127.7 63.9 %copy-start = (f32[512,32]{0,1:T(8,128)S(1)}, f32[512,32]{0,1:T(8,128)}, u32[]{:S(2)}) copy-start(f32[512,32]{0,1:T(8,128)} %reduce-scatter.3.cloned.1.call-done) | copy-start | bytes 196612
  423.3 200.5 %reduce-scatter.5.cloned.1.call-start = ((), (), s32[]{:S(2)}) async-start(), calls=%async_computation.10 | async-start | bytes 1114112 | tf_op jit(solution)/shard_map/reduce_scatter | solution.py:48
  499.1 23.8 %collective-permute-start = (f32[512,256]{0,1:T(8,128)S(1)}, f32[512,256]{0,1:T(8,128)S(1)}, u32[]{:S(2)}, u32[]{:S(2)}) collective-permute-start(f32[512,256]{0,1:T(8,128)S(1)} %get-tuple-element.10), channel_id=1, source_target_pairs={{0,16},{16,32},{32,48},{48,64},{64,80},{80,96},{96,112},{112,128},... | collective-permute-start | bytes 1572872 | tf_op jit(solution)/shard_map/ppermute | solution.py:14
  527.8 466.4 %all-gather.5.cloned.1.call-start = ((), (), s32[]{:S(2)}) async-start(), calls=%async_computation.11 | async-start | bytes 1114112 | tf_op jit(solution)/shard_map/all_gather | solution.py:68
  626.1 63.9 %copy-start.1 = (f32[512,32]{0,1:T(8,128)S(1)}, f32[512,32]{0,1:T(8,128)}, u32[]{:S(2)}) copy-start(f32[512,32]{0,1:T(8,128)} %reduce-scatter.5.cloned.1.call-done) | copy-start | bytes 196612
  997.6 23.8 %collective-permute-start.1 = (f32[512,256]{0,1:T(8,128)S(1)}, f32[512,256]{0,1:T(8,128)S(1)}, u32[]{:S(2)}, u32[]{:S(2)}) collective-permute-start(f32[512,256]{0,1:T(8,128)S(1)} %get-tuple-element.8), channel_id=1, source_target_pairs={{0,16},{16,32},{32,48},{48,64},{64,80},{80,96},{96,112},{112,128},... | collective-permute-start | bytes 1572872 | tf_op jit(solution)/shard_map/ppermute | solution.py:14
Sparse Core Ops, SparseCore 0:
  13.8 111.5 reduce-scatter.2
  423.4 72.2 all-gather.2
  527.9 95.8 reduce-scatter.4
  921.9 72.1 all-gather.4
